TPU v7x, 512 devices: a whole 4x4x16 slice. The times are simulated.
512 devices in a mesh: ax: 32 (over x_lo, z), az: 16 (over y, x_hi, core).
Axes of the slice: x: 4 (x_hi: 2, x_lo: 2; x = x_hi * 2 + x_lo), y: 4, z: 16, core: 2. Of those that a mesh axis runs over, the one named last changes fastest.
Arguments:
- conserved: float32 [5, 256, 1024, 128], P(None, 'ax', 'az'), may hold values from -0.6 to 3, as said below
- panel_cells: int32 [262144], P(('ax', 'az')), may hold values from 0 to 65535
- panel_counts: int32 [512], P(('ax', 'az')), may hold values from 1 to 512, 131072 in all
- time_bins: int32 [262144, 64], P(('ax', 'az')), may hold values from 0 to 1023
- amplitudes: float32 [262144, 64], P(('ax', 'az')), may hold values from 0.5 to 2
Outputs:
- section: float32 [5, 256, 1024, 128], P(None, 'ax', 'az')
- signal: float32 [64, 1024], P(None, ('ax', 'az'))
Inputs may be any that keep to these rules, and one draw needn't show every extreme that they name: `conserved`: component 0 lies in 0.7 to 1.3, components 1 to 3 in -0.6 to 0.6, component 4 in 2.0 to 3.0. `panel_counts`: some device has exactly 512 live panel slots, each device at least one.
All inputs are finite; a program needn't handle non-finite values.
Results may differ from a plain program's by a relative error of at most 0.000076.
Values sent between devices are 32-bit elements; how exact they have to be, the bound alone decides.
A program may use at most 64 MiB of HBM per device.

v0:
```python
import math
import jax
import jax.numpy as jnp
from jax import lax
from jax.sharding import PartitionSpec as P

AZIMUTH = 1024
CYCLES = 8
OBSERVERS = 64
BINS = 1024
gas_factor = 0.4
time_step = 0.02
ref_pressure = 0.95


def padded_2(value, sides, width, wrap):
    for axis, dim in sides:
        size, length = (lax.axis_size(axis), value.shape[dim])
        up = [(i, (i + 1) % size) for i in range(size if wrap else size - 1)]
        down = [(j, i) for i, j in up]
        last = lax.slice_in_dim(value, length - width, length, axis=dim)
        leading = lax.slice_in_dim(value, 0, width, axis=dim)
        before = lax.ppermute(last, axis, up)
        after = lax.ppermute(leading, axis, down)
        value = jnp.concatenate([before, value, after], axis=dim)
    return value


def primitives(conserved):
    fluid_rho_value = conserved[0]
    axial_vel = conserved[1] / fluid_rho_value
    radial_vel = conserved[2] / fluid_rho_value
    swirl_vel = conserved[3] / fluid_rho_value
    kinetic = 0.5 * (
        conserved[1] * axial_vel + conserved[2] * radial_vel + conserved[3] * swirl_vel
    )
    thermo_stress_level = gas_factor * (conserved[4] - kinetic)
    return jnp.stack([fluid_rho_value, axial_vel, radial_vel, swirl_vel, thermo_stress_level])


def flux_along(primitive, stream_heading):
    fluid_rho_value = primitive[0]
    thermo_stress_level = primitive[4]
    stream_speed = [primitive[1], primitive[2], primitive[3]]
    overall_heat_work = thermo_stress_level / gas_factor + 0.5 * fluid_rho_value * (
        stream_speed[0] * stream_speed[0]
        + stream_speed[1] * stream_speed[1]
        + stream_speed[2] * stream_speed[2]
    )
    holder_buffer = stream_speed[stream_heading]
    divided_pieces = [fluid_rho_value * holder_buffer]
    for entry_number in range(3):
        forcing_contribution = fluid_rho_value * stream_speed[entry_number] * holder_buffer
        if entry_number == stream_heading:
            forcing_contribution = forcing_contribution + thermo_stress_level
        divided_pieces.append(forcing_contribution)
    divided_pieces.append((overall_heat_work + thermo_stress_level) * holder_buffer)
    return jnp.stack(divided_pieces)


def fourth_diff(padded, along_axis, length):
    near_diff = lax.slice_in_dim(padded, 3, length + 3, axis=along_axis) - lax.slice_in_dim(
        padded, 1, length + 1, axis=along_axis
    )
    far_diff = lax.slice_in_dim(padded, 4, length + 4, axis=along_axis) - lax.slice_in_dim(
        padded, 0, length, axis=along_axis
    )
    return (8.0 * near_diff - far_diff) / 12.0


def cycle_weights(length):
    modes = jnp.arange(length // 2 + 1).astype(jnp.float32)
    cutoff = 4.0 * (jnp.arange(CYCLES).astype(jnp.float32) + 1.0)
    return jnp.exp(-((modes[None, :] / cutoff[:, None]) ** 8))


def apply_filter(line_block, cycle_index, length):
    half = length // 2 + 1
    sample = jnp.arange(length)
    modes = jnp.arange(half)
    phase = (sample[:, None] * modes[None, :] % length).astype(jnp.float32) * (
        2.0 * math.pi / length
    )
    cos_table = jnp.cos(phase)
    sin_table = jnp.sin(phase)
    factor = jnp.where((modes == 0) | (modes == length // 2), 1.0, 2.0) / length
    selector = (cycle_index[:, None] == jnp.arange(CYCLES)[None, :]).astype(jnp.float32)
    line_weight = (
        jnp.dot(selector, cycle_weights(length), precision=lax.Precision.HIGHEST) * factor[None, :]
    )
    real_part = jnp.einsum("fln,nm->flm", line_block, cos_table, precision=lax.Precision.HIGHEST)
    imag_part = jnp.einsum("fln,nm->flm", line_block, sin_table, precision=lax.Precision.HIGHEST)
    smooth = jnp.einsum(
        "flm,nm->fln", real_part * line_weight[None], cos_table, precision=lax.Precision.HIGHEST
    )
    smooth = smooth + jnp.einsum(
        "flm,nm->fln", imag_part * line_weight[None], sin_table, precision=lax.Precision.HIGHEST
    )
    return smooth


def on_device(conserved, panel_cells, panel_counts, time_bins, amplitudes):
    planes_dev = conserved.shape[1]
    sector = conserved.shape[2]
    radial_all = conserved.shape[3]
    primitive = primitives(conserved)
    radius = jnp.arange(radial_all).astype(jnp.float32) + 0.5
    dtheta = 2.0 * math.pi / AZIMUTH
    axial_flux = flux_along(primitive, 0)
    swirl_flux = flux_along(primitive, 2)
    padded_x = padded_2(axial_flux, (("ax", 1),), 2, False)
    padded_t = padded_2(swirl_flux, (("az", 2),), 2, True)
    radial_flux = flux_along(primitive, 1)
    padded_r = jnp.pad(radial_flux * radius, ((0, 0), (0, 0), (0, 0), (2, 2)))
    tendency = -fourth_diff(padded_x, 1, planes_dev)
    tendency = tendency - fourth_diff(padded_r, 3, radial_all) / radius
    tendency = tendency - fourth_diff(padded_t, 2, sector) / (radius * dtheta)
    fluid_rho_value = primitive[0]
    radial_vel = primitive[2]
    swirl_vel = primitive[3]
    thermo_stress_level = primitive[4]
    zeros_field = jnp.zeros_like(fluid_rho_value)
    source = jnp.stack(
        [
            zeros_field,
            zeros_field,
            (thermo_stress_level + fluid_rho_value * swirl_vel * swirl_vel) / radius,
            -fluid_rho_value * radial_vel * swirl_vel / radius,
            zeros_field,
        ]
    )
    raw_section = conserved + time_step * (tendency + source)
    inner = raw_section[..., :CYCLES]
    lines = jnp.transpose(inner, (0, 1, 3, 2)).reshape(5, planes_dev * CYCLES, sector)
    line_block = lax.all_to_all(lines, "az", split_axis=1, concat_axis=2, tiled=True)
    line_count = line_block.shape[1]
    cycle_index = (lax.axis_index("az") * line_count + jnp.arange(line_count)) % CYCLES
    smooth = apply_filter(line_block, cycle_index, AZIMUTH)
    filtered = lax.all_to_all(smooth, "az", split_axis=2, concat_axis=1, tiled=True)
    filtered = jnp.transpose(filtered.reshape(5, planes_dev, CYCLES, sector), (0, 1, 3, 2))
    section = jnp.concatenate([filtered, raw_section[..., CYCLES:]], axis=3)
    slot_count = panel_cells.shape[0]
    live = jnp.arange(slot_count) < panel_counts[0]
    sampled = jnp.where(live, thermo_stress_level.reshape(-1)[panel_cells] - ref_pressure, 0.0)
    contrib = sampled[:, None] * amplitudes
    segment = jnp.arange(OBSERVERS)[None, :] * BINS + time_bins
    partial_signal = jax.ops.segment_sum(
        contrib.reshape(-1), segment.reshape(-1), num_segments=OBSERVERS * BINS
    )
    signal = lax.psum_scatter(
        partial_signal.reshape(OBSERVERS, BINS), ("ax", "az"), scatter_dimension=1, tiled=True
    )
    return (section, signal)


def solution(mesh):
    placed = (
        P(None, "ax", "az", None),
        P(("ax", "az")),
        P(("ax", "az")),
        P(("ax", "az"), None),
        P(("ax", "az"), None),
    )
    return jax.shard_map(
        on_device,
        mesh=mesh,
        in_specs=placed,
        out_specs=(P(None, "ax", "az", None), P(None, ("ax", "az"))),
        check_vma=False,
    )
```

profile of v0, /device:TPU:4, one launch (start us, length us, event | category | flops | bytes accessed | tf_op | source)
XLA Modules:
  0.0 676.7 jit_solution(17818139211325658250)
XLA Ops:
  7.2 1.8 constant_dynamic-update-slice_fusion
  10.4 2.2 add_dynamic-update-slice_fusion.1
  13.7 3.1 gather_fusion
  17.5 171.1 %scatter_custom_fusion = f32[65536]{0:T(1024)S(1)} fusion(s32[32768]{0:T(1024)S(1)} %reshape.97, f32[32768]{0:T(1024)S(1)} %reshape.99, f32[]{:T(128)} %constant.31.clone.1), kind=kCustom, calls=%fused_computation.96 | custom fusion | flops 32768 | bytes 262148 | tf_op jit(solution)/shard_map/scatter-add | solution.py:147
  193.6 1.1 copy-done.2
  194.7 1.9 collective-permute-start.2
  197.3 2.4 collective-permute-start.3
  199.7 2.0 fusion.90
  201.7 1.3 collective-permute-start
  202.9 5.3 collective-permute-start.1
  213.6 4.0 multiply_add_fusion
  219.2 10.9 %all-to-all-start = ((f32[16,1,1280]{2,1,0:T(1,128)}), f32[16,1,1280]{2,1,0:T(1,128)S(1)}, u32[]{:S(2)}, u32[]{:S(2)}) async-start(f32[16,1,1280]{2,1,0:T(1,128)} %reshape.112), calls=%async_computation | async-start | bytes 163840 | tf_op jit(solution)/shard_map/all_to_all | solution.py:135
  230.3 4.7 all-to-all-done
  236.6 10.2 %fusion.45 = f32[5,4,513]{2,0,1:T(8,128)S(1)} fusion(f32[5,4,1024]{2,1,0:T(4,128)S(1)} %all_to_all.27, f32[4,513]{1,0:T(4,128)S(1)} %convolution_multiply_fusion), kind=kOutput, calls=%fused_computation.65 | convolution fusion | flops 133439504 | bytes 131168 | tf_op jit(solution)/shard_map/fln,nm->flm/dot_general | solution.py:92
  246.8 10.1 %fusion.42 = f32[5,4,513]{2,0,1:T(8,128)S(1)} fusion(f32[5,4,1024]{2,1,0:T(4,128)S(1)} %all_to_all.27, f32[4,513]{1,0:T(4,128)S(1)} %convolution_multiply_fusion), kind=kOutput, calls=%fused_computation.64 | convolution fusion | flops 133439504 | bytes 131168 | tf_op jit(solution)/shard_map/fln,nm->flm/dot_general | solution.py:91
  256.9 9.7 %fusion.3 = f32[5,4,1024]{2,0,1:T(8,128)S(1)} fusion(f32[5,4,513]{2,0,1:T(8,128)S(1)} %fusion.45), kind=kOutput, calls=%fused_computation.12 | convolution fusion | flops 133429248 | bytes 122960 | tf_op jit(solution)/shard_map/flm,nm->fln/dot_general | solution.py:96
  266.6 9.6 %fusion.39 = f32[5,4,1024]{2,0,1:T(8,128)S(1)} fusion(f32[5,4,1024]{2,0,1:T(8,128)S(1)} %fusion.3, f32[5,4,513]{2,0,1:T(8,128)S(1)} %fusion.42), kind=kOutput, calls=%fused_computation.63 | convolution fusion | flops 133449728 | bytes 204880 | tf_op jit(solution)/shard_map/flm,nm->fln/dot_general | solution.py:93
  276.2 1.8 copy.79
  277.9 4.4 reshape.114
  282.3 6.2 all-to-all-start.1
  288.5 371.6 %all-reduce.4.cloned.1.call-done = f32[64,1024]{1,0:T(8,128)} async-done(((f32[64,1024]{1,0:T(8,128)}), f32[64,1024]{1,0:T(8,128)}) %all-reduce.4.cloned.1.call-update) | async-done | bytes 262160
  662.8 2.6 reshape.115
  665.4 1.6 copy.87
  668.4 1.5 pad_maximum_fusion.4
  (82 shorter events, 20.8 us)
Async XLA Ops:
  7.2 653.0 %all-reduce.4.cloned.1.call-start = ((), (), s32[]{:S(2)}) async-start(), calls=%async_computation.2 | async-start | bytes 524288
  10.4 2.2 copy-start
  13.7 3.2 copy-start.5
  13.7 3.4 copy-start.6
  189.4 1.5 copy-start.1
  189.4 4.2 copy-start.7
  193.6 1.1 copy-start.2
  193.6 17.0 %copy-start.4 = (f32[5,8,64,128]{3,2,1,0:T(8,128)S(1)}, f32[5,8,64,128]{3,2,1,0:T(8,128)}, u32[]{:S(2)}) copy-start(f32[5,8,64,128]{3,2,1,0:T(8,128)} %get-tuple-element.40) | copy-start | bytes 3932164
  194.7 17.4 %collective-permute-start.2 = (f32[5,8,2,128]{3,1,2,0:T(8,128)S(1)}, f32[5,8,2,128]{3,1,2,0:T(8,128)S(1)}, u32[]{:S(2)}, u32[]{:S(2)}) collective-permute-start(f32[5,8,2,128]{3,1,2,0:T(8,128)S(1)} %copy.70), channel_id=1, source_target_pairs={{1,0},{2,1},{3,2},{4,3},{5,4},{6,5},{7,6},{8,7},{9,8},{10,9},{11,1... | collective-permute-start | bytes 122888 | tf_op jit(solution)/shard_map/ppermute | solution.py:24
  197.3 14.9 %collective-permute-start.3 = (f32[5,8,2,128]{3,1,2,0:T(8,128)}, f32[5,8,2,128]{3,1,2,0:T(8,128)}, u32[]{:S(2)}, u32[]{:S(2)}) collective-permute-start(f32[5,8,2,128]{3,1,2,0:T(8,128)} %copy.72), channel_id=1, source_target_pairs={{0,1},{1,2},{2,3},{3,4},{4,5},{5,6},{6,7},{7,8},{8,9},{9,10},{10,1... | collective-permute-start | bytes 122888 | tf_op jit(solution)/shard_map/ppermute | solution.py:23
  201.7 11.3 %collective-permute-start = (f32[5,2,64,128]{3,2,1,0:T(8,128)}, f32[5,2,64,128]{3,2,1,0:T(8,128)S(1)}, u32[]{:S(2)}, u32[]{:S(2)}) collective-permute-start(f32[5,2,64,128]{3,2,1,0:T(8,128)} %get-tuple-element.35), channel_id=1, source_target_pairs={{16,0},{32,16},{48,32},{64,48},{80,64},{96,80},{112,96},{128,112},... | collective-permute-start | bytes 983048 | tf_op jit(solution)/shard_map/ppermute | solution.py:24
  202.9 10.7 %collective-permute-start.1 = (f32[5,2,64,128]{3,2,1,0:T(8,128)}, f32[5,2,64,128]{3,2,1,0:T(8,128)}, u32[]{:S(2)}, u32[]{:S(2)}) collective-permute-start(f32[5,2,64,128]{3,2,1,0:T(8,128)} %get-tuple-element.36), channel_id=1, source_target_pairs={{0,16},{16,32},{32,48},{48,64},{64,80},{80,96},{96,112},{112,128},... | collective-permute-start | bytes 983048 | tf_op jit(solution)/shard_map/ppermute | solution.py:23
  210.6 3.0 copy-start.3
  210.6 3.0 copy-start.8
  210.6 3.0 copy-start.11
  217.7 12.3 %copy-start.9 = (f32[513]{0:T(1024)S(1)}, f32[513]{0:T(1024)}, u32[]{:S(2)}) copy-start(f32[513]{0:T(1024)} %iota_convert_fusion) | copy-start | bytes 6160
  217.7 12.3 %copy-start.10 = (f32[513]{0:T(1024)S(1)}, f32[513]{0:T(1024)}, u32[]{:S(2)}) copy-start(f32[513]{0:T(1024)} %select_multiply_fusion) | copy-start | bytes 6160
  217.8 12.3 %copy-start.12 = (s32[4]{0:T(128)S(1)}, s32[4]{0:T(128)}, u32[]{:S(2)}) copy-start(s32[4]{0:T(128)} %and_select_fusion) | copy-start | bytes 52
  217.8 12.3 %copy-start.13 = (f32[8]{0:T(128)S(1)}, f32[8]{0:T(128)}, u32[]{:S(2)}) copy-start(f32[8]{0:T(128)} %add_multiply_fusion) | copy-start | bytes 100
  219.2 15.8 %all-to-all-start = ((f32[16,1,1280]{2,1,0:T(1,128)}), f32[16,1,1280]{2,1,0:T(1,128)S(1)}, u32[]{:S(2)}, u32[]{:S(2)}) async-start(f32[16,1,1280]{2,1,0:T(1,128)} %reshape.112), calls=%async_computation | async-start | bytes 163840 | tf_op jit(solution)/shard_map/all_to_all | solution.py:135
  282.3 379.7 %all-to-all-start.1 = ((f32[16,1,1280]{2,1,0:T(1,128)}), f32[16,1,1280]{2,1,0:T(1,128)S(1)}, u32[]{:S(2)}, u32[]{:S(2)}) async-start(f32[16,1,1280]{2,1,0:T(1,128)} %reshape.114), calls=%async_computation.1 | async-start | bytes 163840 | tf_op jit(solution)/shard_map/all_to_all | solution.py:139
Sparse Core Ops, SparseCore 0:
  189.5 470.5 all-reduce.3
where the time goes:
time: 677 us
  waiting for transfers between devices  377 us (56%)
  other arithmetic  191 us (28%)
  matrix products  39.7 us (6%)
  starting transfers between devices  28 us (4%)
  local copies, waits for them, and re-layouts  25.5 us (4%)
  between operations  15.1 us (2%)
    unnamed x2, waiting for transfers between devices  372 us
    scatter-add x1, other arithmetic, on_device(): jax.ops.segment_sum(contrib.reshape(-1), segment.reshape(-1), num_segment...  171 us
  transfers between devices with their start and end apart: 7, of which 3 were waited for; matrix products, arithmetic and copies ran while one was open for 10% of the time, Pallas kernels for 0%

commit v1 on v0

--- a/solution.py
+++ b/solution.py
@@ -132,7 +132,9 @@
     raw_section = conserved + time_step * (tendency + source)
     inner = raw_section[..., :CYCLES]
     lines = jnp.transpose(inner, (0, 1, 3, 2)).reshape(5, planes_dev * CYCLES, sector)
-    line_block = lax.all_to_all(lines, "az", split_axis=1, concat_axis=2, tiled=True)
+    line_block = jnp.concatenate(
+        lax.all_to_all(jnp.stack(jnp.split(lines, lax.axis_size("az"), axis=1)), "az", 0, 0), axis=2
+    )
     line_count = line_block.shape[1]
     cycle_index = (lax.axis_index("az") * line_count + jnp.arange(line_count)) % CYCLES
     smooth = apply_filter(line_block, cycle_index, AZIMUTH)

time: 677 us -> 677 us (level)
  starting transfers between devices: 28 us -> 36.1 us
  transfers between devices with their start and end apart: 7 -> 7, of which waited for: 3 -> 3; matrix products, arithmetic and copies ran while one was open for 10% -> 9% of each run, Pallas kernels for 0% -> 0%
where the time goes in v1:
time: 677 us
  waiting for transfers between devices  374 us (55%)
  other arithmetic  187 us (28%)
  matrix products  39.7 us (6%)
  starting transfers between devices  36.1 us (5%)
  local copies, waits for them, and re-layouts  24.5 us (4%)
  between operations  15.3 us (2%)
    unnamed x2, waiting for transfers between devices  368 us
    scatter-add x1, other arithmetic, on_device(): jax.ops.segment_sum(contrib.reshape(-1), segment.reshape(-1), num_segment...  171 us
    all_to_all x1, starting transfers between devices, on_device(): lax.all_to_all(jnp.stack(jnp.split(lines, lax.axis_size('az'), axis=1)),...  16.2 us
  transfers between devices with their start and end apart: 7, of which 3 were waited for; matrix products, arithmetic and copies ran while one was open for 9% of the time, Pallas kernels for 0%

profile of v1, /device:TPU:4, one launch (start us, length us, event | category | flops | bytes accessed | tf_op | source)
XLA Modules:
  0.0 676.8 jit_solution(9232927676452415728)
XLA Ops:
  9.9 1.8 constant_dynamic-update-slice_fusion
  13.6 3.1 gather_fusion
  17.1 171.1 %scatter_custom_fusion = f32[65536]{0:T(1024)S(1)} fusion(s32[32768]{0:T(1024)S(1)} %reshape.105, f32[32768]{0:T(1024)S(1)} %reshape.107, f32[]{:T(128)} %constant.31.clone.1), kind=kCustom, calls=%fused_computation.93 | custom fusion | flops 32768 | bytes 262148 | tf_op jit(solution)/shard_map/scatter-add | solution.py:149
  191.3 1.1 multiply_dynamic-update-slice_fusion.4
  192.5 2.1 fusion.88
  194.6 1.3 collective-permute-start
  195.8 5.3 collective-permute-start.1
  202.4 1.9 collective-permute-start.3
  204.3 5.1 collective-permute-start.2
  209.8 1.3 collective-permute-done.2
  211.2 4.2 multiply_add_fusion
  217.0 16.2 %all-to-all-start = ((f32[16,1,1280]{2,1,0:T(1,128)}), f32[16,1,1280]{2,1,0:T(1,128)S(1)}, u32[]{:S(2)}, u32[]{:S(2)}) async-start(f32[16,1,1280]{2,1,0:T(1,128)} %reshape.121), calls=%async_computation | async-start | bytes 163840 | tf_op jit(solution)/shard_map/all_to_all | solution.py:136
  233.4 4.7 all-to-all-done
  239.7 10.1 %fusion.45 = f32[5,4,513]{2,0,1:T(8,128)S(1)} fusion(f32[5,4,1024]{2,0,1:T(8,128)S(1)} %reshape.117, f32[4,513]{1,0:T(4,128)S(1)} %convolution_multiply_fusion), kind=kOutput, calls=%fused_computation.65 | convolution fusion | flops 133439504 | bytes 131168 | tf_op jit(solution)/shard_map/fln,nm->flm/dot_general | solution.py:92
  249.9 10.1 %fusion.42 = f32[5,4,513]{2,0,1:T(8,128)S(1)} fusion(f32[5,4,1024]{2,0,1:T(8,128)S(1)} %reshape.117, f32[4,513]{1,0:T(4,128)S(1)} %convolution_multiply_fusion), kind=kOutput, calls=%fused_computation.64 | convolution fusion | flops 133439504 | bytes 131168 | tf_op jit(solution)/shard_map/fln,nm->flm/dot_general | solution.py:91
  260.0 9.7 %fusion.3 = f32[5,4,1024]{2,0,1:T(8,128)S(1)} fusion(f32[5,4,513]{2,0,1:T(8,128)S(1)} %fusion.45), kind=kOutput, calls=%fused_computation.12 | convolution fusion | flops 133429248 | bytes 122960 | tf_op jit(solution)/shard_map/flm,nm->fln/dot_general | solution.py:96
  269.6 9.6 %fusion.39 = f32[5,4,1024]{2,0,1:T(8,128)S(1)} fusion(f32[5,4,1024]{2,0,1:T(8,128)S(1)} %fusion.3, f32[5,4,513]{2,0,1:T(8,128)S(1)} %fusion.42), kind=kOutput, calls=%fused_computation.63 | convolution fusion | flops 133449728 | bytes 204880 | tf_op jit(solution)/shard_map/flm,nm->fln/dot_general | solution.py:93
  279.2 1.8 copy.77
  281.0 4.4 reshape.123
  285.4 6.2 all-to-all-start.1
  291.6 368.3 %all-reduce.4.cloned.1.call-done = f32[64,1024]{1,0:T(8,128)} async-done(((f32[64,1024]{1,0:T(8,128)}), f32[64,1024]{1,0:T(8,128)}) %all-reduce.4.cloned.1.call-update) | async-done | bytes 262160
  661.3 1.5 slice.118
  663.6 2.6 reshape.124
  668.5 1.5 pad_maximum_fusion.4
  (88 shorter events, 16.6 us)
Async XLA Ops:
  7.2 4.5 copy-start
  7.2 652.7 %all-reduce.4.cloned.1.call-start = ((), (), s32[]{:S(2)}) async-start(), calls=%async_computation.2 | async-start | bytes 524288
  13.6 3.2 copy-start.8
  188.9 1.5 copy-start.2
  192.5 8.7 %copy-start.5 = (f32[5,8,64,128]{3,2,1,0:T(8,128)S(1)}, f32[5,8,64,128]{3,2,1,0:T(8,128)}, u32[]{:S(2)}) copy-start(f32[5,8,64,128]{3,2,1,0:T(8,128)} %get-tuple-element.18) | copy-start | bytes 3932164
  194.6 16.6 %collective-permute-start = (f32[5,2,64,128]{3,2,1,0:T(8,128)}, f32[5,2,64,128]{3,2,1,0:T(8,128)}, u32[]{:S(2)}, u32[]{:S(2)}) collective-permute-start(f32[5,2,64,128]{3,2,1,0:T(8,128)} %get-tuple-element.35), channel_id=1, source_target_pairs={{16,0},{32,16},{48,32},{64,48},{80,64},{96,80},{112,96},{128,112},... | collective-permute-start | bytes 983048 | tf_op jit(solution)/shard_map/ppermute | solution.py:24
  195.8 15.3 %collective-permute-start.1 = (f32[5,2,64,128]{3,2,1,0:T(8,128)}, f32[5,2,64,128]{3,2,1,0:T(8,128)}, u32[]{:S(2)}, u32[]{:S(2)}) collective-permute-start(f32[5,2,64,128]{3,2,1,0:T(8,128)} %get-tuple-element.36), channel_id=1, source_target_pairs={{0,16},{16,32},{32,48},{48,64},{64,80},{80,96},{96,112},{112,128},... | collective-permute-start | bytes 983048 | tf_op jit(solution)/shard_map/ppermute | solution.py:23
  201.3 1.1 copy-start.3
  202.4 7.4 %collective-permute-start.3 = (f32[5,8,2,128]{3,1,2,0:T(8,128)S(1)}, f32[5,8,2,128]{3,1,2,0:T(8,128)S(1)}, u32[]{:S(2)}, u32[]{:S(2)}) collective-permute-start(f32[5,8,2,128]{3,1,2,0:T(8,128)S(1)} %copy.71), channel_id=1, source_target_pairs={{0,1},{1,2},{2,3},{3,4},{4,5},{5,6},{6,7},{7,8},{8,9},{9,10},{10,1... | collective-permute-start | bytes 122888 | tf_op jit(solution)/shard_map/ppermute | solution.py:23
  204.3 6.8 %collective-permute-start.2 = (f32[5,8,2,128]{3,1,2,0:T(8,128)S(1)}, f32[5,8,2,128]{3,1,2,0:T(8,128)S(1)}, u32[]{:S(2)}, u32[]{:S(2)}) collective-permute-start(f32[5,8,2,128]{3,1,2,0:T(8,128)S(1)} %copy.69), channel_id=1, source_target_pairs={{1,0},{2,1},{3,2},{4,3},{5,4},{6,5},{7,6},{8,7},{9,8},{10,9},{11,1... | collective-permute-start | bytes 122888 | tf_op jit(solution)/shard_map/ppermute | solution.py:24
  209.5 1.6 copy-start.4
  209.5 1.6 copy-start.6
  209.5 1.6 copy-start.7
  217.0 21.2 %all-to-all-start = ((f32[16,1,1280]{2,1,0:T(1,128)}), f32[16,1,1280]{2,1,0:T(1,128)S(1)}, u32[]{:S(2)}, u32[]{:S(2)}) async-start(f32[16,1,1280]{2,1,0:T(1,128)} %reshape.121), calls=%async_computation | async-start | bytes 163840 | tf_op jit(solution)/shard_map/all_to_all | solution.py:136
  285.4 377.4 %all-to-all-start.1 = ((f32[16,1,1280]{2,1,0:T(1,128)}), f32[16,1,1280]{2,1,0:T(1,128)S(1)}, u32[]{:S(2)}, u32[]{:S(2)}) async-start(f32[16,1,1280]{2,1,0:T(1,128)} %reshape.123), calls=%async_computation.1 | async-start | bytes 163840 | tf_op jit(solution)/shard_map/all_to_all | solution.py:141
  667.2 1.3 copy-start.1
Sparse Core Ops, SparseCore 0:
  189.1 470.7 all-reduce.3
